TPU v7x, 32 devices: a whole 2x2x4 slice. The times are simulated.
32 devices in a mesh: grp: 2 (over core), dev: 16 (over z, y, x).
Axes of the slice: x: 2, y: 2, z: 4, core: 2. Of those that a mesh axis runs over, the one named last changes fastest.
Arguments:
- embeds_t: bfloat16 [1024, 131072], P(None, ('grp', 'dev'))
- shard_counts: int32 [32], P(('grp', 'dev')), may hold values from 512 to 4096, as said below
- assignments: int32 [64, 131072], P('dev', 'grp'), may hold values from 0 to 255
Outputs:
- whitened: bfloat16 [1024, 131072], P('dev', 'grp')
- factor: float32 [1024, 1024], replicated
- centroids: float32 [64, 16, 256], P('dev')
Inputs may be any that keep to these rules, and one draw needn't show every extreme that they name: `shard_counts`: each shard holds between 512 and 4096 rows in its leading slots; one shard is full and one holds exactly 512.
All inputs are finite; a program needn't handle non-finite values.
Results may differ from a plain program's by a relative error of at most 0.0029.
Values may be sent and summed in bfloat16 or wider, within the bound.
A program may use at most 192 MiB of HBM per device.

v0:
```python
import jax
import jax.numpy as jnp
from jax import lax
from jax.sharding import PartitionSpec as P

CENT = 256


def body(embeds_t, shard_counts, assignments):
    row_dev = embeds_t.shape[1]
    counts_all = lax.all_gather(shard_counts, ("grp", "dev"), axis=0, tiled=True)
    slot_ids = jnp.arange(row_dev, dtype=jnp.int32)
    valid_slots = (slot_ids < shard_counts[0]).astype(jnp.float32)
    total_rows = jnp.sum(counts_all).astype(jnp.float32)
    as_float = embeds_t.astype(jnp.float32)
    col_sum = lax.psum(jnp.sum(as_float * valid_slots[None, :], axis=1), ("grp", "dev"))
    col_mean = col_sum / total_rows
    centred = (as_float - col_mean[:, None]) * valid_slots[None, :]
    gram_part = lax.dot_general(
        centred,
        centred,
        (((1,), (1,)), ((), ())),
        precision=lax.Precision.HIGHEST,
        preferred_element_type=jnp.float32,
    )
    gram_sum = lax.psum(gram_part, ("grp", "dev"))
    factor = jnp.linalg.cholesky(gram_sum / (total_rows - 1.0))
    white_local = lax.linalg.triangular_solve(factor, centred, left_side=True, lower=True).astype(
        jnp.bfloat16
    )
    owned_rows = lax.all_to_all(white_local, "dev", split_axis=0, concat_axis=1, tiled=True)
    sub_dev = assignments.shape[0]
    sub_width = owned_rows.shape[0] // sub_dev
    group_rows = owned_rows.shape[1]
    num_dev = lax.axis_size("dev")
    limits = lax.dynamic_slice_in_dim(counts_all, lax.axis_index("grp") * num_dev, num_dev)
    valid_rows = (slot_ids[None, :] < limits[:, None]).reshape(-1)
    blk_rows = min(4096, group_rows)
    centre_ids = jnp.arange(CENT, dtype=jnp.int32)

    def add_block(blk_index, carry):
        cent_sums, cent_counts = carry
        row_start = blk_index * blk_rows
        sub_rows = lax.dynamic_slice_in_dim(owned_rows, row_start, blk_rows, 1).reshape(
            sub_dev, sub_width, blk_rows
        )
        sub_assign = lax.dynamic_slice_in_dim(assignments, row_start, blk_rows, 1)
        row_ok = lax.dynamic_slice_in_dim(valid_rows, row_start, blk_rows, 0)
        one_hot = (
            (sub_assign[:, :, None] == centre_ids[None, None, :]) & row_ok[None, :, None]
        ).astype(jnp.bfloat16)
        cent_sums = cent_sums + jnp.einsum(
            "swb,sbc->swc", sub_rows, one_hot, preferred_element_type=jnp.float32
        )
        cent_counts = cent_counts + jnp.sum(one_hot, axis=1, dtype=jnp.float32)
        return (cent_sums, cent_counts)

    start_sums = jnp.zeros((sub_dev, sub_width, CENT), jnp.float32)
    start_counts = jnp.zeros((sub_dev, CENT), jnp.float32)
    cent_sums, cent_counts = lax.fori_loop(
        0, group_rows // blk_rows, add_block, (start_sums, start_counts)
    )
    cent_sums, cent_counts = lax.psum((cent_sums, cent_counts), "grp")
    centroids = cent_sums / (cent_counts[:, None, :] + 1.0)
    return (owned_rows, factor, centroids)


def solution(mesh):
    return jax.shard_map(
        body,
        mesh=mesh,
        in_specs=(P(None, ("grp", "dev")), P(("grp", "dev")), P("dev", "grp")),
        out_specs=(P("dev", "grp"), P(), P("dev", None, None)),
        check_vma=False,
    )
```

profile of v0, /device:TPU:0, one launch (start us, length us, event | category | flops | bytes accessed | tf_op | source)
XLA Modules:
  0.0 1166.8 jit_solution(4400866553339165679)
XLA Ops:
  8.0 41.9 %all-reduce.1 = s32[32]{0:T(128)S(1)} all-reduce(s32[32]{0:T(128)S(1)} %dynamic-update-slice.47), channel_id=1, replica_groups=mesh['grp'=2,'dev'=16] {'grp','dev'}, use_global_device_ids=true, to_apply=%add.1 | all-reduce | flops 32 | bytes 256
  51.2 5.1 fusion.11
  56.3 40.1 %psum.28 = f32[1024]{0:T(1024)S(1)} all-reduce(f32[1024]{0:T(1024)S(1)} %fusion.11), channel_id=1, replica_groups=mesh['grp'=2,'dev'=16] {'grp','dev'}, use_global_device_ids=true, to_apply=%region_1.0 | all-reduce | flops 1024 | bytes 8192 | tf_op jit(solution)/shard_map/psum | solution.py:16
  96.4 63.0 %fusion.86 = f32[1024,1024]{0,1:T(8,128)} fusion(bf16[1024,4096]{1,0:T(8,128)(2,1)} %param.5, f32[1024]{0:T(1024)S(1)} %broadcast_divide_fusion.2, f32[4096]{0:T(1024)S(1)} %fusion.82), kind=kOutput, calls=%fused_computation.182 | convolution fusion | flops 51552190464 | bytes 12603392 | tf_op jit(solution)/shard_map/dot_general | solution.py:19
  159.5 12.1 %fusion.12 = f32[1024,4096]{1,0:T(8,128)} fusion(bf16[1024,4096]{1,0:T(8,128)(2,1)} %param.5, f32[1024]{0:T(1024)S(1)} %broadcast_divide_fusion.2, f32[4096]{0:T(1024)S(1)} %fusion.82), kind=kLoop, calls=%fused_computation.17 | loop fusion | flops 12582912 | bytes 25186304 | tf_op jit(solution)/shard_map/mul | solution.py:18
  171.7 130.9 %all-reduce.5.cloned.1.call-done = f32[1024,1024]{0,1:T(8,128)} async-done(((f32[1024,1024]{0,1:T(8,128)}), f32[1024,1024]{0,1:T(8,128)}) %all-reduce.5.cloned.1.call-update) | async-done | bytes 4194320 | tf_op jit(solution)/shard_map/psum | solution.py:26
  302.6 5.0 broadcast_divide_fusion
  307.6 5.8 copy.7
  313.4 4.5 fusion.37
  319.9 11.7 %cholesky.223 = f32[128,128]{1,0:T(8,128)S(1)} custom-call(f32[128,128]{1,0:T(8,128)S(1)} %cholesky.580), custom_call_target="Cholesky" | custom-call | tf_op jit(solution)/shard_map/jit(cholesky)/cholesky | solution.py:27
  331.6 9.8 custom-call.62
  347.9 11.9 %cholesky.244 = f32[128,128]{1,0:T(8,128)S(1)} custom-call(f32[128,128]{1,0:T(8,128)S(1)} %cholesky.584), custom_call_target="Cholesky" | custom-call | tf_op jit(solution)/shard_map/jit(cholesky)/cholesky | solution.py:27
  360.4 9.8 custom-call.63
  373.5 11.7 %cholesky.468 = f32[128,128]{1,0:T(8,128)S(1)} custom-call(f32[128,128]{1,0:T(8,128)S(1)} %cholesky.589), custom_call_target="Cholesky" | custom-call | tf_op jit(solution)/shard_map/jit(cholesky)/cholesky | solution.py:27
  386.5 9.8 custom-call.64
  399.8 11.9 %cholesky.487 = f32[128,128]{1,0:T(8,128)S(1)} custom-call(f32[128,128]{1,0:T(8,128)S(1)} %cholesky.594), custom_call_target="Cholesky" | custom-call | tf_op jit(solution)/shard_map/jit(cholesky)/cholesky | solution.py:27
  413.1 9.8 custom-call.65
  426.3 11.7 %cholesky.506 = f32[128,128]{1,0:T(8,128)S(1)} custom-call(f32[128,128]{1,0:T(8,128)S(1)} %cholesky.599), custom_call_target="Cholesky" | custom-call | tf_op jit(solution)/shard_map/jit(cholesky)/cholesky | solution.py:27
  439.3 10.2 custom-call.66
  452.8 11.7 %cholesky.526 = f32[128,128]{1,0:T(8,128)S(1)} custom-call(f32[128,128]{1,0:T(8,128)S(1)} %cholesky.604), custom_call_target="Cholesky" | custom-call | tf_op jit(solution)/shard_map/jit(cholesky)/cholesky | solution.py:27
  465.8 9.8 custom-call.67
  478.7 11.9 %cholesky.546 = f32[128,128]{1,0:T(8,128)S(1)} custom-call(f32[128,128]{1,0:T(8,128)S(1)} %cholesky.609), custom_call_target="Cholesky" | custom-call | tf_op jit(solution)/shard_map/jit(cholesky)/cholesky | solution.py:27
  491.9 9.8 custom-call.68
  504.4 11.7 %cholesky.564 = f32[128,128]{1,0:T(8,128)S(1)} custom-call(f32[128,128]{1,0:T(8,128)S(1)} %convolution_subtract_fusion.11), custom_call_target="Cholesky" | custom-call | tf_op jit(solution)/shard_map/jit(cholesky)/cholesky | solution.py:27
  523.2 6.7 fusion.38
  529.9 22.5 %while.17 = (s32[]{:T(128)}, f32[1024,1024]{1,0:T(8,128)}, s32[8,2]{0,1:T(2,128)S(1)}, f32[8,128,128]{2,1,0:T(8,128)S(1)}, s32[]{:T(128)}) while((s32[]{:T(128)}, f32[1024,1024]{1,0:T(8,128)}, s32[8,2]{0,1:T(2,128)S(1)}, f32[8,128,128]{2,1,0:T(8,128)S(1)}, s32[]{:T(128)}) %tuple.85), condition=%wide.while_cond, body=%wide.while_body.sunk | while | flops 2 | bytes 131181 | solution.py:28
  552.4 78.8 %custom-call.69 = f32[8,128,128]{1,2,0:T(8,128)S(1)} custom-call(f32[8,128,128]{2,1,0:T(8,128)S(1)} %get-tuple-element.137), custom_call_target="InvertDiagBlocksLowerTriangular" | custom-call | tf_op jit(solution)/shard_map/triangular_solve | solution.py:28
  631.3 4.6 convert_dynamic-update-slice_fusion.6
  653.0 5.2 fusion.27
  661.2 6.4 fusion.30
  685.2 9.1 convolution_subtract_fusion.1
  700.5 9.8 convolution_subtract_fusion
  715.6 11.8 %convolution_subtract_fusion.4 = f32[128,4096]{1,0:T(8,128)S(1)} fusion(f32[896,4096]{1,0:T(8,128)} %constant_dynamic-update-slice_fusion.11, f32[1024,4096]{1,0:T(8,128)S(1)} %bitcast.117, f32[1024,1024]{1,0:T(8,128)} %get-tuple-element.357), kind=kOutput, calls=%fused_computation.36 | convolution fusion | flops 5637668864 | bytes 19333120 | tf_op jit(solution)/shard_map/triangular_solve | solution.py:28
  731.1 4.9 all-to-all-start
  736.4 152.4 %all-to-all-done = bf16[16,64,4096]{2,1,0:T(8,128)(2,1)} async-done(((bf16[16,64,4096]{2,1,0:T(8,128)(2,1)}), bf16[16,64,4096]{2,1,0:T(8,128)(2,1)}, u32[]{:S(2)}, u32[]{:S(2)}) %all-to-all-start) | async-done | bytes 8388640 | tf_op jit(solution)/shard_map/all_to_all | solution.py:31
  888.8 7.9 copy.10
  896.7 208.9 %while.18 = (s32[]{:T(128)}, f32[4,16,256]{2,1,0:T(8,128)S(1)}, f32[4,256]{1,0:T(4,128)S(1)}, bf16[64,65536]{1,0:T(8,128)(2,1)}, s32[4,65536]{1,0:T(4,128)}, /*i...) while((s32[]{:T(128)}, f32[4,16,256]{2,1,0:T(8,128)S(1)}, ...), condition=%wide.region_22.23_spmd.clone, body=%wide.region_20.22_spmd.clone.sunk | while | flops 163611648 | bytes 1999018 | solution.py:60
  898.6 6.7 fusion.113
  905.3 4.3 convert_reduce_fusion.2
  911.7 6.7 fusion.113
  918.4 4.3 convert_reduce_fusion.2
  924.7 6.7 fusion.113
  931.5 4.3 convert_reduce_fusion.2
  937.8 6.7 fusion.113
  944.5 4.3 convert_reduce_fusion.2
  950.8 6.7 fusion.113
  957.6 4.3 convert_reduce_fusion.2
  963.9 6.7 fusion.113
  970.6 4.3 convert_reduce_fusion.2
  976.9 6.7 fusion.113
  990.0 6.7 fusion.113
  996.7 4.3 convert_reduce_fusion.2
  1003.1 6.7 fusion.113
  1016.1 6.7 fusion.113
  1029.2 6.7 fusion.113
  1035.9 4.3 convert_reduce_fusion.2
  1042.2 6.7 fusion.113
  1055.3 6.7 fusion.113
  1062.0 4.3 convert_reduce_fusion.2
  1068.3 6.7 fusion.113
  1081.4 6.7 fusion.113
  1094.5 6.7 fusion.113
  1101.2 4.3 convert_reduce_fusion.2
  1108.1 50.1 %all-reduce.7.cloned.1.call-done = f32[4,16,256]{2,1,0:T(8,128)} async-done(((f32[4,16,256]{2,1,0:T(8,128)}), f32[4,16,256]{2,1,0:T(8,128)}) %all-reduce.7.cloned.1.call-update) | async-done | bytes 65552 | tf_op jit(solution)/shard_map/psum | solution.py:63
  (182 shorter events, 174.2 us)
Async XLA Ops:
  7.2 295.4 %all-reduce.5.cloned.1.call-start = ((), (), s32[]{:S(2)}) async-start(), calls=%async_computation.1 | async-start | bytes 8388608 | tf_op jit(solution)/shard_map/psum | solution.py:26
  317.9 2.0 copy-start
  631.3 27.0 %copy-start.1 = (f32[8,128,128]{1,2,0:T(8,128)}, f32[8,128,128]{1,2,0:T(8,128)S(1)}, u32[]{:S(2)}) copy-start(f32[8,128,128]{1,2,0:T(8,128)S(1)} %custom-call.69) | copy-start | bytes 1572868
  635.9 17.1 %slice-start = ((s8[16777216]{0:T(1024)(128)(4,1)}), s8[4194304]{0:T(1024)(128)(4,1)S(1)}, s32[]{:S(2)}) async-start(s8[16777216]{0:T(1024)(128)(4,1)} %bitcast.116), calls=%async_computation.3 | async-start | bytes 8388608
  639.3 13.7 %slice-start.1 = ((s8[16777216]{0:T(1024)(128)(4,1)}), s8[4194304]{0:T(1024)(128)(4,1)S(1)}, s32[]{:S(2)}) async-start(s8[16777216]{0:T(1024)(128)(4,1)} %bitcast.116), calls=%async_computation.4 | async-start | bytes 8388608
  643.0 10.0 slice-start.2
  645.9 7.1 slice-start.3
  731.1 157.6 %all-to-all-start = ((bf16[16,64,4096]{2,1,0:T(8,128)(2,1)}), bf16[16,64,4096]{2,1,0:T(8,128)(2,1)}, u32[]{:S(2)}, u32[]{:S(2)}) async-start(bf16[16,64,4096]{2,1,0:T(8,128)(2,1)} %bitcast.24), calls=%async_computation | async-start | bytes 16777216 | tf_op jit(solution)/shard_map/all_to_all | solution.py:31
  736.1 422.2 %all-reduce.7.cloned.1.call-start = ((), (), s32[]{:S(2)}) async-start(), calls=%async_computation.2 | async-start | bytes 131072 | tf_op jit(solution)/shard_map/psum | solution.py:63
  1105.6 2.5 copy-start.2
Sparse Core Ops, SparseCore 0:
  159.6 142.9 all-reduce.4
  1108.2 49.9 all-reduce.6
where the time goes:
time: 1180 us; the launch traced here: 1170 us
  other arithmetic  356 us (30%)
  waiting for transfers between devices  333 us (28%)
  matrix products  272 us (23%)
  local copies, waits for them, and re-layouts  92.9 us (8%)
  blocking collectives  84.6 us (7%)
  between operations  21 us (2%)
    another operation x30, other arithmetic, body(): factor = jnp.linalg.cholesky(gram_sum / (total_rows - 1.0))  172 us
    all_to_all x1, waiting for transfers between devices, body(): lax.all_to_all(white_local, 'dev', split_axis=0, concat_axis=1, tiled=True)  152 us
    psum x1, waiting for transfers between devices, body(): gram_sum = lax.psum(gram_part, ('grp', 'dev'))  131 us
    dot_general x16, matrix products, add_block(): jnp.einsum('swb,sbc->swc', sub_rows, one_hot, preferred_element_type=jnp....  108 us
    another operation x3, other arithmetic, body(): lax.linalg.triangular_solve(factor, centred, left_side=True, lower=True)  85.5 us
    another operation x15, matrix products, body(): lax.linalg.triangular_solve(factor, centred, left_side=True, lower=True)  78.5 us
    reduce_sum x16, other arithmetic, add_block(): cent_counts = cent_counts + jnp.sum(one_hot, axis=1, dtype=jnp.float32)  69.4 us
    dot_general x1, matrix products, body(): lax.dot_general(centred, centred, (((1,), (1,)), ((), ())), precision=lax...  63 us
  transfers between devices with their start and end apart: 3, of which 3 were waited for; matrix products, arithmetic and copies ran while one was open for 1% of the time, Pallas kernels for 0%

commit v1 on v0

--- a/solution.py
+++ b/solution.py
@@ -2,6 +2,7 @@
 import jax.numpy as jnp
 from jax import lax
 from jax.sharding import PartitionSpec as P
+from jax.lax import psum
 
 CENT = 256
 
@@ -23,7 +24,9 @@
         precision=lax.Precision.HIGHEST,
         preferred_element_type=jnp.float32,
     )
-    gram_sum = lax.psum(gram_part, ("grp", "dev"))
+    gram_sum = gram_part
+    for it in ("dev", "grp"):
+        gram_sum = psum(gram_sum, it)
     factor = jnp.linalg.cholesky(gram_sum / (total_rows - 1.0))
     white_local = lax.linalg.triangular_solve(factor, centred, left_side=True, lower=True).astype(
         jnp.bfloat16

time: 1180 us -> 1240 us (1.051)
  waiting for transfers between devices: 333 us -> 394 us
    psum x1 -> x2, waiting for transfers between devices: 131 us -> 185 us  [body(): gram_sum = psum(gram_sum, it)]
  transfers between devices with their start and end apart: 3 -> 4, of which waited for: 3 -> 4; matrix products, arithmetic and copies ran while one was open for 1% -> 1% of each run, Pallas kernels for 0% -> 0%
where the time goes in v1:
time: 1240 us; the launch traced here: 1230 us
  waiting for transfers between devices  394 us (32%)
  other arithmetic  358 us (29%)
  matrix products  272 us (22%)
  local copies, waits for them, and re-layouts  92.9 us (7%)
  blocking collectives  84.5 us (7%)
  between operations  20.7 us (2%)
    psum x2, waiting for transfers between devices, body(): gram_sum = psum(gram_sum, it)  185 us
    another operation x30, other arithmetic, body(): factor = jnp.linalg.cholesky(gram_sum / (total_rows - 1.0))  172 us
    all_to_all x1, waiting for transfers between devices, body(): lax.all_to_all(white_local, 'dev', split_axis=0, concat_axis=1, tiled=True)  159 us
    dot_general x16, matrix products, add_block(): jnp.einsum('swb,sbc->swc', sub_rows, one_hot, preferred_element_type=jnp....  108 us
    another operation x3, other arithmetic, body(): lax.linalg.triangular_solve(factor, centred, left_side=True, lower=True)  85.5 us
    another operation x15, matrix products, body(): lax.linalg.triangular_solve(factor, centred, left_side=True, lower=True)  78.5 us
    reduce_sum x16, other arithmetic, add_block(): cent_counts = cent_counts + jnp.sum(one_hot, axis=1, dtype=jnp.float32)  69.4 us
    dot_general x1, matrix products, body(): lax.dot_general(centred, centred, (((1,), (1,)), ((), ())), precision=lax...  63 us
  transfers between devices with their start and end apart: 4, of which 4 were waited for; matrix products, arithmetic and copies ran while one was open for 1% of the time, Pallas kernels for 0%

profile of v1, /device:TPU:0, one launch (start us, length us, event | category | flops | bytes accessed | tf_op | source)
XLA Modules:
  0.0 1230.2 jit_solution(2512784921018566874)
XLA Ops:
  8.0 41.9 %all-reduce.1 = s32[32]{0:T(128)S(1)} all-reduce(s32[32]{0:T(128)S(1)} %dynamic-update-slice.47), channel_id=1, replica_groups=mesh['grp'=2,'dev'=16] {'grp','dev'}, use_global_device_ids=true, to_apply=%add.1 | all-reduce | flops 32 | bytes 256
  51.2 5.1 fusion.11
  56.3 40.1 %psum.35 = f32[1024]{0:T(1024)S(1)} all-reduce(f32[1024]{0:T(1024)S(1)} %fusion.11), channel_id=1, replica_groups=mesh['grp'=2,'dev'=16] {'grp','dev'}, use_global_device_ids=true, to_apply=%region_1.0 | all-reduce | flops 1024 | bytes 8192 | tf_op jit(solution)/shard_map/psum | solution.py:17
  96.4 63.0 %fusion.86 = f32[1024,1024]{0,1:T(8,128)} fusion(bf16[1024,4096]{1,0:T(8,128)(2,1)} %param.5, f32[1024]{0:T(1024)S(1)} %broadcast_divide_fusion.2, f32[4096]{0:T(1024)S(1)} %fusion.82), kind=kOutput, calls=%fused_computation.182 | convolution fusion | flops 51552190464 | bytes 12603392 | tf_op jit(solution)/shard_map/dot_general | solution.py:20
  159.5 169.0 %all-reduce.6.cloned.1.call-done = f32[1024,1024]{0,1:T(8,128)} async-done(((f32[1024,1024]{0,1:T(8,128)}), f32[1024,1024]{0,1:T(8,128)}) %all-reduce.6.cloned.1.call-update) | async-done | bytes 4194320 | tf_op jit(solution)/shard_map/psum | solution.py:29
  328.6 14.0 %fusion.12 = f32[1024,4096]{1,0:T(8,128)} fusion(bf16[1024,4096]{1,0:T(8,128)(2,1)} %param.5, f32[1024]{0:T(1024)S(1)} %broadcast_divide_fusion.2, f32[4096]{0:T(1024)S(1)} %fusion.82), kind=kLoop, calls=%fused_computation.17 | loop fusion | flops 12582912 | bytes 25186304 | tf_op jit(solution)/shard_map/mul | solution.py:19
  342.6 15.6 %all-reduce.8.cloned.1.call-done = f32[1024,1024]{0,1:T(8,128)} async-done(((f32[1024,1024]{0,1:T(8,128)}), f32[1024,1024]{0,1:T(8,128)}) %all-reduce.8.cloned.1.call-update) | async-done | bytes 4194320 | tf_op jit(solution)/shard_map/psum | solution.py:29
  358.2 5.0 broadcast_divide_fusion
  363.3 5.8 copy.7
  369.0 4.5 fusion.37
  375.5 11.7 cholesky.223
  387.3 9.8 custom-call.62
  403.5 11.9 cholesky.244
  416.0 9.8 custom-call.63
  429.2 11.7 cholesky.468
  442.1 9.8 custom-call.64
  455.4 11.9 cholesky.487
  468.7 9.8 custom-call.65
  481.9 11.7 cholesky.506
  495.0 10.2 custom-call.66
  508.4 11.7 cholesky.526
  521.4 9.8 custom-call.67
  534.3 11.9 cholesky.546
  547.4 9.8 custom-call.68
  559.9 11.7 cholesky.564
  578.6 6.7 fusion.38
  585.4 22.5 %while.17 = (s32[]{:T(128)}, f32[1024,1024]{1,0:T(8,128)}, s32[8,2]{0,1:T(2,128)S(1)}, f32[8,128,128]{2,1,0:T(8,128)S(1)}, s32[]{:T(128)}) while((s32[]{:T(128)}, f32[1024,1024]{1,0:T(8,128)}, s32[8,2]{0,1:T(2,128)S(1)}, f32[8,128,128]{2,1,0:T(8,128)S(1)}, s32[]{:T(128)}) %tuple.85), condition=%wide.while_cond, body=%wide.while_body.sunk | while | flops 2 | bytes 131181 | solution.py:31
  607.9 78.8 %custom-call.69 = f32[8,128,128]{1,2,0:T(8,128)S(1)} custom-call(f32[8,128,128]{2,1,0:T(8,128)S(1)} %get-tuple-element.137), custom_call_target="InvertDiagBlocksLowerTriangular" | custom-call | tf_op jit(solution)/shard_map/triangular_solve | solution.py:31
  686.7 4.6 convert_dynamic-update-slice_fusion.6
  708.5 5.2 fusion.27
  716.7 6.4 fusion.30
  740.7 9.1 convolution_subtract_fusion.1
  756.0 9.8 convolution_subtract_fusion
  771.1 11.8 convolution_subtract_fusion.4
  786.6 6.8 all-to-all-start
  793.8 158.9 %all-to-all-done = bf16[16,64,4096]{2,1,0:T(8,128)(2,1)} async-done(((bf16[16,64,4096]{2,1,0:T(8,128)(2,1)}), bf16[16,64,4096]{2,1,0:T(8,128)(2,1)}, u32[]{:S(2)}, u32[]{:S(2)}) %all-to-all-start) | async-done | bytes 8388640 | tf_op jit(solution)/shard_map/all_to_all | solution.py:34
  952.7 7.9 copy.10
  960.6 208.9 %while.18 = (s32[]{:T(128)}, f32[4,16,256]{2,1,0:T(8,128)S(1)}, f32[4,256]{1,0:T(4,128)S(1)}, bf16[64,65536]{1,0:T(8,128)(2,1)}, s32[4,65536]{1,0:T(4,128)}, /*i...) while((s32[]{:T(128)}, f32[4,16,256]{2,1,0:T(8,128)S(1)}, ...), condition=%wide.region_23.24_spmd.clone, body=%wide.region_21.23_spmd.clone.sunk | while | flops 163611648 | bytes 1999018 | solution.py:63
  962.5 6.7 fusion.113
  969.3 4.3 convert_reduce_fusion.2
  975.6 6.7 fusion.113
  982.3 4.3 convert_reduce_fusion.2
  988.6 6.7 fusion.113
  995.4 4.3 convert_reduce_fusion.2
  1001.7 6.7 fusion.113
  1008.4 4.3 convert_reduce_fusion.2
  1014.7 6.7 fusion.113
  1027.8 6.7 fusion.113
  1040.9 6.7 fusion.113
  1047.6 4.3 convert_reduce_fusion.2
  1053.9 6.7 fusion.113
  1067.0 6.7 fusion.113
  1073.7 4.3 convert_reduce_fusion.2
  1080.0 6.7 fusion.113
  1093.1 6.7 fusion.113
  1099.8 4.3 convert_reduce_fusion.2
  1106.1 6.7 fusion.113
  1119.2 6.7 fusion.113
  1132.3 6.7 fusion.113
  1139.0 4.3 convert_reduce_fusion.2
  1145.3 6.7 fusion.113
  1158.4 6.7 fusion.113
  1165.1 4.3 convert_reduce_fusion.2
  1172.0 50.0 %all-reduce.10.cloned.1.call-done = f32[4,16,256]{2,1,0:T(8,128)} async-done(((f32[4,16,256]{2,1,0:T(8,128)}), f32[4,16,256]{2,1,0:T(8,128)}) %all-reduce.10.cloned.1.call-update) | async-done | bytes 65552 | tf_op jit(solution)/shard_map/psum | solution.py:66
  (185 shorter events, 178.4 us)
Async XLA Ops:
  7.2 321.4 %all-reduce.6.cloned.1.call-start = ((), (), s32[]{:S(2)}) async-start(), calls=%async_computation.1 | async-start | bytes 8388608 | tf_op jit(solution)/shard_map/psum | solution.py:29
  159.5 198.7 %all-reduce.8.cloned.1.call-start = ((), (), s32[]{:S(2)}) async-start(), calls=%async_computation.2 | async-start | bytes 8388608 | tf_op jit(solution)/shard_map/psum | solution.py:29
  373.5 2.0 copy-start
  686.7 27.0 %copy-start.1 = (f32[8,128,128]{1,2,0:T(8,128)}, f32[8,128,128]{1,2,0:T(8,128)S(1)}, u32[]{:S(2)}) copy-start(f32[8,128,128]{1,2,0:T(8,128)S(1)} %custom-call.69) | copy-start | bytes 1572868
  691.4 17.1 %slice-start = ((s8[16777216]{0:T(1024)(128)(4,1)}), s8[4194304]{0:T(1024)(128)(4,1)S(1)}, s32[]{:S(2)}) async-start(s8[16777216]{0:T(1024)(128)(4,1)} %bitcast.116), calls=%async_computation.4 | async-start | bytes 8388608
  694.8 13.7 %slice-start.1 = ((s8[16777216]{0:T(1024)(128)(4,1)}), s8[4194304]{0:T(1024)(128)(4,1)S(1)}, s32[]{:S(2)}) async-start(s8[16777216]{0:T(1024)(128)(4,1)} %bitcast.116), calls=%async_computation.5 | async-start | bytes 8388608
  698.4 10.0 slice-start.2
  701.3 7.1 slice-start.3
  786.6 166.1 %all-to-all-start = ((bf16[16,64,4096]{2,1,0:T(8,128)(2,1)}), bf16[16,64,4096]{2,1,0:T(8,128)(2,1)}, u32[]{:S(2)}, u32[]{:S(2)}) async-start(bf16[16,64,4096]{2,1,0:T(8,128)(2,1)} %bitcast.24), calls=%async_computation | async-start | bytes 16777216 | tf_op jit(solution)/shard_map/all_to_all | solution.py:34
  793.5 428.6 %all-reduce.10.cloned.1.call-start = ((), (), s32[]{:S(2)}) async-start(), calls=%async_computation.3 | async-start | bytes 131072 | tf_op jit(solution)/shard_map/psum | solution.py:66
  1169.5 2.5 copy-start.2
Sparse Core Ops, SparseCore 0:
  159.6 168.9 all-reduce.5
  331.0 27.1 all-reduce.7
  1172.1 49.8 all-reduce.9
